TPU v7x, 32 devices: a whole 2x2x4 slice. The times are simulated.
32 devices in a mesh: grp: 2 (over y), row: 8 (over z, core), col: 2 (over x).
Axes of the slice: x: 2, y: 2, z: 4, core: 2. Of those that a mesh axis runs over, the one named last changes fastest.
Arguments:
- pair: bfloat16 [192, 96, 128], P(('grp', 'row'), 'col'), parts along dimension 0, may hold values from -6 to 6
- token_count: int32 [2], P('grp'), parts along dimension 0, may hold values from 72 to 96
- tri_in: bfloat16 [2, 128, 512], replicated, may hold values from -0.5 to 0.5
- tri_gate: bfloat16 [2, 128, 128], replicated, may hold values from -0.5 to 0.5
- tri_out: bfloat16 [2, 128, 128], replicated, may hold values from -0.5 to 0.5
- trans_in: bfloat16 [128, 1024], replicated, may hold values from -0.5 to 0.5
- trans_out: bfloat16 [512, 128], replicated, may hold values from -0.25 to 0.25
Outputs:
- pair_out: bfloat16 [192, 96, 128], P(('grp', 'row'), 'col'), parts along dimension 0
There are 2 independent parts, one for each index of `grp`. A program takes and returns all parts, laid end to end along the dimension named above; an argument that names none is the same for every part. Nothing has to cross between parts.
Inputs may be any that keep to these rules, and one draw needn't show every extreme that they name: `token_count`: the number of real tokens of the complex; pair entries with either token index at or past it are padding.
All inputs are finite; a program needn't handle non-finite values.
Results may differ from a plain program's by a relative error of at most 0.015.
Values may be sent and summed in bfloat16 or wider, within the bound.
No kernel may reach another device: no remote copies, remote signals or barrier semaphores. Data moves between devices by JAX's collectives and lax.ppermute only.
A program may use at most 64 MiB of HBM per device.

v0:
```python
import jax
import jax.numpy as jnp
from jax import lax
from jax.sharding import PartitionSpec as P


def layer_norm(values, along):
    average = jnp.mean(values, axis=along, keepdims=True)
    centred = values - average
    spread = jnp.mean(centred * centred, axis=along, keepdims=True)
    return centred * lax.rsqrt(spread + 1e-05)


def contract_rows(left_side, right_side):
    return jnp.einsum("hik,hjk->hij", left_side, right_side, preferred_element_type=jnp.float32)


def contract_columns(left_side, right_side):
    return jnp.einsum("hki,hkj->hij", left_side, right_side, preferred_element_type=jnp.float32)


def body(pair, token_count, tri_in, tri_gate, tri_out, trans_in, trans_out):
    tile_rows, tile_cols, pair_width = pair.shape
    hidden = tri_out.shape[1]
    ffn_width = trans_out.shape[0]
    row_place = lax.axis_index("row")
    col_place = lax.axis_index("col")
    row_first = row_place * tile_rows
    col_first = col_place * tile_cols
    token_limit = token_count[0]
    row_keep = (row_first + jnp.arange(tile_rows, dtype=jnp.int32) < token_limit).astype(
        jnp.float32
    )
    col_keep = (col_first + jnp.arange(tile_cols, dtype=jnp.int32) < token_limit).astype(
        jnp.float32
    )
    keep_mask = row_keep[:, None] * col_keep[None, :]

    def project(stream, which_side):
        normed = layer_norm(stream.astype(jnp.float32), 2).astype(jnp.bfloat16)
        weight = tri_in[which_side].reshape(pair_width, 4, hidden)
        projected = jnp.einsum("ijc,cgh->ghij", normed, weight, preferred_element_type=jnp.float32)
        left_side = (keep_mask * jax.nn.sigmoid(projected[2]) * projected[0]).astype(jnp.bfloat16)
        right_side = (keep_mask * jax.nn.sigmoid(projected[3]) * projected[1]).astype(jnp.bfloat16)
        gate_value = jax.nn.sigmoid(
            jnp.dot(normed, tri_gate[which_side], preferred_element_type=jnp.float32)
        )
        return (left_side, right_side, gate_value)

    def finish(stream, mixed_sum, gate_value, which_side):
        normed = layer_norm(mixed_sum, 0).astype(jnp.bfloat16)
        update = gate_value * jnp.einsum(
            "hij,hc->ijc", normed, tri_out[which_side], preferred_element_type=jnp.float32
        )
        return (stream.astype(jnp.float32) + keep_mask[:, :, None] * update).astype(jnp.bfloat16)

    left_side, right_side, gate_value = project(pair, 0)
    partial_rows = contract_rows(left_side, lax.all_gather(right_side, "row", axis=1, tiled=True))
    mixed_sum = lax.psum_scatter(partial_rows, "col", scatter_dimension=2, tiled=True)
    stream = finish(pair, mixed_sum, gate_value, 0)
    left_side, right_side, gate_value = project(stream, 1)
    left_rows = lax.all_gather(left_side, "col", axis=2, tiled=True)
    column_strip = lax.all_to_all(left_rows, "row", split_axis=2, concat_axis=1, tiled=True)
    mixed_sum = contract_columns(
        column_strip, lax.all_gather(right_side, "row", axis=1, tiled=True)
    )
    stream = finish(stream, mixed_sum, gate_value, 1)
    normed = layer_norm(stream.astype(jnp.float32), 2).astype(jnp.bfloat16)
    inner_sum = jnp.dot(normed, trans_in, preferred_element_type=jnp.float32)
    activation = (jax.nn.silu(inner_sum[..., :ffn_width]) * inner_sum[..., ffn_width:]).astype(
        jnp.bfloat16
    )
    update = jnp.dot(activation, trans_out, preferred_element_type=jnp.float32)
    return (stream.astype(jnp.float32) + keep_mask[:, :, None] * update).astype(jnp.bfloat16)


def solution(mesh):
    placed = (P(("grp", "row"), "col", None), P("grp"), P(), P(), P(), P(), P())
    return jax.shard_map(
        body, mesh=mesh, in_specs=placed, out_specs=P(("grp", "row"), "col", None), check_vma=False
    )
```

profile of v0, /device:TPU:0, one launch (start us, length us, event | category | flops | bytes accessed | tf_op | source)
XLA Modules:
  0.0 121.3 jit_solution(946812768014044533)
XLA Ops:
  7.2 1.1 convert_reduce_fusion
  8.3 1.2 fusion.21
  9.5 1.6 %fusion.72 = (bf16[1,128,512]{2,1,0:T(8,128)(2,1)}, bf16[1,128,512]{2,1,0:T(8,128)(2,1)S(1)}) fusion(bf16[2,128,512]{2,1,0:T(8,128)(2,1)} %param.9), kind=kLoop, calls=%fused_computation.108 | loop fusion | bytes 524288 | tf_op jit(solution)/shard_map/slice | solution.py:41
  11.2 0.1 copy.110
  11.3 0.1 broadcast_multiply_fusion.5
  11.4 0.4 convolution_bitcast_fusion.1
  11.8 0.9 fusion.38
  12.7 0.0 all-gather.3.cloned.1.call-update
  12.7 0.0 reduce-scatter.2.cloned.1.call-start
  12.7 1.2 %copy.84 = bf16[128,12,48]{2,1,0:T(8,128)(2,1)} copy(bf16[128,12,48]{0,2,1:T(8,128)(2,1)S(1)} %get-tuple-element.8) | data formatting | bytes 294912 | tf_op jit(solution)/shard_map/convert_element_type | solution.py:43
  14.0 24.4 %all-gather.3.cloned.1.call-done = bf16[128,96,48]{0,2,1:T(8,128)(2,1)} async-done(((bf16[128,12,48]{0,2,1:T(8,128)(2,1)}), bf16[128,96,48]{0,2,1:T(8,128)(2,1)}) %all-gather.3.cloned.1.call-update) | async-done | bytes 1179664 | tf_op jit(solution)/shard_map/all_gather | solution.py:58
  38.3 5.3 %copy.85 = bf16[128,96,48]{2,1,0:T(8,128)(2,1)S(1)} copy(bf16[128,96,48]{0,2,1:T(8,128)(2,1)} %all-gather.3.cloned.1.call-done) | data formatting | bytes 2359296 | tf_op jit(solution)/shard_map/all_gather | solution.py:58
  43.6 3.7 %fusion.76 = f32[128,12,96]{2,1,0:T(8,128)} fusion(bf16[128,12,48]{2,1,0:T(8,128)(2,1)} %copy.84, bf16[128,96,48]{2,1,0:T(8,128)(2,1)S(1)} %copy.85), kind=kOutput, calls=%fused_computation.112 | convolution fusion | flops 14155776 | bytes 1916928 | tf_op jit(solution)/shard_map/hik,hjk->hij/dot_general | solution.py:15
  47.4 2.7 %copy.86 = f32[128,12,96]{0,1,2:T(8,128)} copy(f32[128,12,96]{2,1,0:T(8,128)} %fusion.76) | data formatting | bytes 1179648 | tf_op jit(solution)/shard_map/hik,hjk->hij/dot_general | solution.py:15
  50.1 0.0 reduce-scatter.2.cloned.1.call-update
  50.2 0.0 all-gather.5.cloned.1.call-start
  50.2 0.1 copy.114
  50.4 0.3 fusion.11
  50.7 16.7 %reduce-scatter.2.cloned.1.call-done = f32[128,12,48]{0,1,2:T(8,128)} async-done(((f32[128,12,96]{0,1,2:T(8,128)}), f32[128,12,48]{0,1,2:T(8,128)}) %reduce-scatter.2.cloned.1.call-update) | async-done | bytes 294928 | tf_op jit(solution)/shard_map/reduce_scatter | solution.py:59
  67.5 1.2 %reduce_sum.92 = f32[12,48]{0,1:T(8,128)S(1)} reduce(f32[128,12,48]{0,1,2:T(8,128)} %reduce-scatter.2.cloned.1.call-done, f32[]{:T(128)} %constant.32.clone.1), dimensions={0}, to_apply=%region_3.0 | reduce | flops 73152 | bytes 297220 | tf_op jit(solution)/shard_map/reduce_sum | solution.py:8
  68.7 0.1 copy.87
  68.8 0.1 copy.88
  68.9 1.3 %multiply_reduce_fusion.1 = f32[12,48]{0,1:T(8,128)S(1)} fusion(f32[128,12,48]{0,1,2:T(8,128)} %reduce-scatter.2.cloned.1.call-done, f32[12,48]{0,1:T(8,128)S(1)} %copy.88), kind=kLoop, calls=%fused_computation.31 | loop fusion | flops 220608 | bytes 299520 | tf_op jit(solution)/shard_map/reduce_sum | solution.py:10
  70.2 0.1 copy.89
  70.3 0.1 copy.90
  70.4 0.3 multiply_convert_fusion.1
  70.7 0.3 fusion.73
  71.0 0.3 multiply_reduce_fusion.3
  71.3 0.4 convolution_bitcast_fusion
  71.7 0.9 fusion.24
  72.6 6.1 %all_gather.10 = bf16[128,12,96]{0,2,1:T(8,128)(2,1)S(1)} all-gather(bf16[128,12,48]{0,2,1:T(8,128)(2,1)S(1)} %get-tuple-element.6), channel_id=1, replica_groups=mesh['grp'=2,'row'=8,'col'=2] {'col'}, dimensions={2}, use_global_device_ids=true | all-gather | bytes 442368 | tf_op jit(solution)/shard_map/all_gather | solution.py:62
  78.6 0.9 copy.95
  79.5 4.6 %all-to-all-start = ((bf16[128,12,96]{0,1,2:T(8,128)(2,1)}), bf16[128,12,96]{0,1,2:T(8,128)(2,1)S(1)}, u32[]{:S(2)}, u32[]{:S(2)}) async-start(bf16[128,12,96]{0,1,2:T(8,128)(2,1)} %copy.95), calls=%async_computation.1 | async-start | bytes 786432 | tf_op jit(solution)/shard_map/all_to_all | solution.py:63
  84.1 1.1 fusion.8
  85.2 17.1 %all-to-all-done = bf16[128,12,96]{0,1,2:T(8,128)(2,1)S(1)} async-done(((bf16[128,12,96]{0,1,2:T(8,128)(2,1)}), bf16[128,12,96]{0,1,2:T(8,128)(2,1)S(1)}, u32[]{:S(2)}, u32[]{:S(2)}) %all-to-all-start) | async-done | bytes 294944 | tf_op jit(solution)/shard_map/all_to_all | solution.py:63
  102.3 0.1 all_to_all.16
  102.4 1.2 %copy.98 = bf16[128,96,12]{1,2,0:T(8,128)(2,1)} copy(bf16[128,96,12]{0,1,2:T(8,128)(2,1)S(1)} %all_to_all.16) | data formatting | bytes 589824 | tf_op jit(solution)/shard_map/all_to_all | solution.py:63
  103.7 5.3 %copy.99 = bf16[128,96,48]{2,1,0:T(8,128)(2,1)S(1)} copy(bf16[128,96,48]{0,2,1:T(8,128)(2,1)} %all-gather.5.cloned.1.call-done) | data formatting | bytes 2359296 | tf_op jit(solution)/shard_map/all_gather | solution.py:65
  109.0 2.0 %fusion.74 = (f32[12,48]{1,0:T(8,128)S(1)}, f32[128,12,48]{2,1,0:T(8,128)S(1)}) fusion(bf16[128,96,12]{1,2,0:T(8,128)(2,1)} %copy.98, bf16[128,96,48]{2,1,0:T(8,128)(2,1)S(1)} %copy.99), kind=kOutput, calls=%fused_computation.110 | convolution fusion | flops 14228928 | bytes 1771776 | tf_op jit(solution)/shard_map/hki,hkj->hij/dot_general | solution.py:19
  111.0 0.2 multiply_reduce_fusion
  111.2 0.1 multiply_convert_fusion
  111.3 0.6 copy-done.2
  111.9 0.1 copy-done.6
  112.0 0.4 fusion.75
  112.4 0.3 multiply_reduce_fusion.2
  112.7 0.5 fusion.53
  113.3 0.4 copy-done.16
  113.6 1.1 fusion.14
  (49 shorter events, 0.2 us)
Async XLA Ops:
  6.5 106.2 %copy-start = (bf16[128,1024]{1,0:T(8,128)(2,1)S(1)}, bf16[128,1024]{1,0:T(8,128)(2,1)}, u32[]{:S(2)}) copy-start(bf16[128,1024]{1,0:T(8,128)(2,1)} %param.12) | copy-start | bytes 786436
  6.5 4.9 %copy-start.4 = (bf16[12,48,128]{2,1,0:T(8,128)(2,1)S(1)}, bf16[12,48,128]{2,1,0:T(8,128)(2,1)}, u32[]{:S(2)}) copy-start(bf16[12,48,128]{2,1,0:T(8,128)(2,1)} %param.7) | copy-start | bytes 442372
  6.5 31.8 %all-gather.3.cloned.1.call-start = ((), (), s32[]{:S(2)}) async-start(), calls=%async_computation.2 | async-start | bytes 1327104 | tf_op jit(solution)/shard_map/all_gather | solution.py:58
  8.3 3.5 %copy-start.10 = (f32[12,48]{1,0:T(8,128)}, f32[12,48]{1,0:T(8,128)S(1)}, u32[]{:S(2)}) copy-start(f32[12,48]{1,0:T(8,128)S(1)} %broadcast_multiply_fusion.4) | copy-start | bytes 6916
  9.5 3.1 %copy-start.14 = (f32[12,48]{1,0:T(8,128)}, f32[12,48]{1,0:T(8,128)S(1)}, u32[]{:S(2)}) copy-start(f32[12,48]{1,0:T(8,128)S(1)} %add_rsqrt_fusion.4) | copy-start | bytes 6916
  11.4 1.2 %copy-start.7 = (f32[12,48]{1,0:T(8,128)}, f32[12,48]{1,0:T(8,128)S(1)}, u32[]{:S(2)}) copy-start(f32[12,48]{1,0:T(8,128)S(1)} %broadcast_multiply_fusion.5) | copy-start | bytes 6916
  12.7 54.8 %reduce-scatter.2.cloned.1.call-start = ((), (), s32[]{:S(2)}) async-start(), calls=%async_computation.3 | async-start | bytes 1179648 | tf_op jit(solution)/shard_map/reduce_scatter | solution.py:59
  47.4 2.8 %copy-start.5 = (bf16[1,128,512]{2,1,0:T(8,128)(2,1)S(1)}, bf16[1,128,512]{2,1,0:T(8,128)(2,1)}, u32[]{:S(2)}) copy-start(bf16[1,128,512]{2,1,0:T(8,128)(2,1)} %get-tuple-element.9) | copy-start | bytes 393220
  47.4 2.9 %copy-start.11 = (f32[12,48]{1,0:T(8,128)S(1)}, f32[12,48]{1,0:T(8,128)}, u32[]{:S(2)}) copy-start(f32[12,48]{1,0:T(8,128)} %copy-done.10) | copy-start | bytes 6916
  47.4 2.9 %copy-start.15 = (f32[12,48]{1,0:T(8,128)S(1)}, f32[12,48]{1,0:T(8,128)}, u32[]{:S(2)}) copy-start(f32[12,48]{1,0:T(8,128)} %copy-done.14) | copy-start | bytes 6916
  47.4 3.0 %copy-start.17 = (bf16[2,128,128]{2,1,0:T(8,128)(2,1)S(1)}, bf16[2,128,128]{2,1,0:T(8,128)(2,1)}, u32[]{:S(2)}) copy-start(bf16[2,128,128]{2,1,0:T(8,128)(2,1)} %param.10) | copy-start | bytes 196612
  50.2 53.5 %all-gather.5.cloned.1.call-start = ((), (), s32[]{:S(2)}) async-start(), calls=%async_computation.4 | async-start | bytes 1327104 | tf_op jit(solution)/shard_map/all_gather | solution.py:65
  50.7 19.9 %copy-start.8 = (f32[12,48]{1,0:T(8,128)S(1)}, f32[12,48]{1,0:T(8,128)}, u32[]{:S(2)}) copy-start(f32[12,48]{1,0:T(8,128)} %copy-done.7) | copy-start | bytes 6916
  50.7 19.9 %copy-start.12 = (bf16[2,128,128]{2,1,0:T(8,128)(2,1)S(1)}, bf16[2,128,128]{2,1,0:T(8,128)(2,1)}, u32[]{:S(2)}) copy-start(bf16[2,128,128]{2,1,0:T(8,128)(2,1)} %param.11) | copy-start | bytes 196612
  67.5 2.9 %copy-start.3 = (f32[128,12,48]{0,1,2:T(8,128)S(1)}, f32[128,12,48]{0,1,2:T(8,128)}, u32[]{:S(2)}) copy-start(f32[128,12,48]{0,1,2:T(8,128)} %reduce-scatter.2.cloned.1.call-done) | copy-start | bytes 884740
  71.0 13.1 %copy-start.1 = (f32[12,48,128]{2,1,0:T(8,128)}, f32[12,48,128]{2,1,0:T(8,128)S(1)}, u32[]{:S(2)}) copy-start(f32[12,48,128]{2,1,0:T(8,128)S(1)} %get-tuple-element.12) | copy-start | bytes 884740
  79.5 22.8 %all-to-all-start = ((bf16[128,12,96]{0,1,2:T(8,128)(2,1)}), bf16[128,12,96]{0,1,2:T(8,128)(2,1)S(1)}, u32[]{:S(2)}, u32[]{:S(2)}) async-start(bf16[128,12,96]{0,1,2:T(8,128)(2,1)} %copy.95), calls=%async_computation.1 | async-start | bytes 786432 | tf_op jit(solution)/shard_map/all_to_all | solution.py:63
  111.0 1.0 copy-start.2
  111.0 1.0 copy-start.6
  111.0 1.0 copy-start.9
  111.0 1.0 copy-start.13
  112.7 0.9 copy-start.16
Sparse Core Ops, SparseCore 0:
  12.8 25.4 all-gather.2
  50.3 17.1 reduce-scatter.1
  72.7 30.0 all-gather.4
where the time goes:
time: 122 us; the launch traced here: 121 us
  waiting for transfers between devices  58.2 us (48%)
  local copies, waits for them, and re-layouts  20.1 us (16%)
  between operations  14.2 us (12%)
  matrix products  10.2 us (8%)
  other arithmetic  7.78 us (6%)
  blocking collectives  6.08 us (5%)
  starting transfers between devices  4.69 us (4%)
    all_gather x2, waiting for transfers between devices, body(): lax.all_gather(right_side, 'row', axis=1, tiled=True)  24.4 us
    all_to_all x1, waiting for transfers between devices, body(): lax.all_to_all(left_rows, 'row', split_axis=2, concat_axis=1, tiled=True)  17.1 us
    reduce_scatter x1, waiting for transfers between devices, body(): lax.psum_scatter(partial_rows, 'col', scatter_dimension=2, tiled=True)  16.7 us
    all_gather x2, local copies, waits for them, and re-layouts, body(): lax.all_gather(right_side, 'row', axis=1, tiled=True)  10.6 us
    all_gather x1, blocking collectives, body(): left_rows = lax.all_gather(left_side, 'col', axis=2, tiled=True)  6.08 us
    all_to_all x1, starting transfers between devices, body(): lax.all_to_all(left_rows, 'row', split_axis=2, concat_axis=1, tiled=True)  4.6 us
    dot_general x1, matrix products, contract_rows(): jnp.einsum('hik,hjk->hij', left_side, right_side, preferred_element_type=...  3.75 us
    reduce_sum x5, other arithmetic, layer_norm(): spread = jnp.mean(centred * centred, axis=along, keepdims=True)  3.23 us
  transfers between devices with their start and end apart: 4, of which 3 were waited for; matrix products, arithmetic and copies ran while one was open for 4% of the time, Pallas kernels for 0%

commit v1 on v0

--- a/solution.py
+++ b/solution.py
@@ -20,6 +20,27 @@
 
 
 def body(pair, token_count, tri_in, tri_gate, tri_out, trans_in, trans_out):
+
+    def turn_scenes(vec):
+        low, built, z_new = (lax.axis_size("row"), lax.axis_index("row"), vec.shape[1])
+        table = list(map(lambda d: (d, (d + 1) % low), range(low)))
+        nodes = list(map(lambda d: (d, (d - 1) % low), range(low)))
+        answer = jnp.zeros((*vec.shape[:1], low * z_new, *vec.shape[2:]), vec.dtype)
+        answer = lax.dynamic_update_slice_in_dim(answer, vec, built * z_new, axis=1)
+        newest = latest = vec
+        passed = low // 2
+        for p in tuple(range(1, passed + 1)):
+            newest = lax.ppermute(newest, "row", table)
+            answer = lax.dynamic_update_slice_in_dim(
+                answer, newest, (built - p) % low * z_new, axis=1
+            )
+            if p < low - passed:
+                latest = lax.ppermute(latest, "row", nodes)
+                answer = lax.dynamic_update_slice_in_dim(
+                    answer, latest, (built + p) % low * z_new, axis=1
+                )
+        return answer
+
     tile_rows, tile_cols, pair_width = pair.shape
     hidden = tri_out.shape[1]
     ffn_width = trans_out.shape[0]
@@ -55,7 +76,7 @@
         return (stream.astype(jnp.float32) + keep_mask[:, :, None] * update).astype(jnp.bfloat16)
 
     left_side, right_side, gate_value = project(pair, 0)
-    partial_rows = contract_rows(left_side, lax.all_gather(right_side, "row", axis=1, tiled=True))
+    partial_rows = contract_rows(left_side, turn_scenes(right_side))
     mixed_sum = lax.psum_scatter(partial_rows, "col", scatter_dimension=2, tiled=True)
     stream = finish(pair, mixed_sum, gate_value, 0)
     left_side, right_side, gate_value = project(stream, 1)

time: 122 us -> 337 us (2.76)
  local copies, waits for them, and re-layouts: 20.1 us -> 235 us
  waiting for transfers between devices: 58.2 us -> 46.3 us
  starting transfers between devices: 4.69 us -> 16.5 us
    dynamic_update_slice x0 -> x8, local copies, waits for them, and re-layouts: none -> 208 us  [the longest x4 114 us: turn_scenes(): lax.dynamic_update_slice_in_dim(answer, newest, (built - p) % low * z_new...]
    all_gather x2 -> x1, waiting for transfers between devices: 24.4 us -> 0.01 us  [body(): lax.all_gather(right_side, 'row', axis=1, tiled=True)]
    ppermute x0 -> x7, local copies, waits for them, and re-layouts: none -> 13.4 us  [the longest x4 7.63 us: turn_scenes(): newest = lax.ppermute(newest, 'row', table)]
    ppermute x0 -> x7, starting transfers between devices: none -> 11.9 us  [the longest x3 11.3 us: turn_scenes(): latest = lax.ppermute(latest, 'row', nodes)]
    ppermute x0 -> x7, waiting for transfers between devices: none -> 10.1 us  [the longest x4 10.1 us: turn_scenes(): newest = lax.ppermute(newest, 'row', table)]
    all_gather x2 -> x1, local copies, waits for them, and re-layouts: 10.6 us -> 5.29 us  [body(): lax.all_gather(right_side, 'row', axis=1, tiled=True)]
  transfers between devices with their start and end apart: 4 -> 10, of which waited for: 3 -> 5; matrix products, arithmetic and copies ran while one was open for 4% -> 59% of each run, Pallas kernels for 0% -> 0%
where the time goes in v1:
time: 337 us; the launch traced here: 336 us
  local copies, waits for them, and re-layouts  235 us (70%)
  waiting for transfers between devices  46.3 us (14%)
  starting transfers between devices  16.5 us (5%)
  between operations  14.7 us (4%)
  matrix products  8.96 us (3%)
  other arithmetic  8.04 us (2%)
  blocking collectives  6.08 us (2%)
    dynamic_update_slice x4, local copies, waits for them, and re-layouts, turn_scenes(): lax.dynamic_update_slice_in_dim(answer, newest, (built - p) % low * z_new...  114 us
    dynamic_update_slice x3, local copies, waits for them, and re-layouts, turn_scenes(): lax.dynamic_update_slice_in_dim(answer, latest, (built + p) % low * z_new...  85.2 us
    reduce_scatter x1, waiting for transfers between devices, body(): lax.psum_scatter(partial_rows, 'col', scatter_dimension=2, tiled=True)  19.1 us
    all_to_all x1, waiting for transfers between devices, body(): lax.all_to_all(left_rows, 'row', split_axis=2, concat_axis=1, tiled=True)  17.1 us
    ppermute x3, starting transfers between devices, turn_scenes(): latest = lax.ppermute(latest, 'row', nodes)  11.3 us
    ppermute x4, waiting for transfers between devices, turn_scenes(): newest = lax.ppermute(newest, 'row', table)  10.1 us
    dynamic_update_slice x1, local copies, waits for them, and re-layouts, turn_scenes(): answer = lax.dynamic_update_slice_in_dim(answer, vec, built * z_new, axis=1)  9.28 us
    ppermute x4, local copies, waits for them, and re-layouts, turn_scenes(): newest = lax.ppermute(newest, 'row', table)  7.63 us
  transfers between devices with their start and end apart: 10, of which 5 were waited for; matrix products, arithmetic and copies ran while one was open for 59% of the time, Pallas kernels for 0%

profile of v1, /device:TPU:0, one launch (start us, length us, event | category | flops | bytes accessed | tf_op | source)
XLA Modules:
  0.0 336.0 jit_solution(18014788370209144609)
XLA Ops:
  7.2 1.1 convert_reduce_fusion
  8.3 1.2 fusion.21
  9.5 1.0 fusion.72
  10.7 1.3 convolution_bitcast_fusion.1
  12.2 0.5 collective-permute-start
  12.8 4.1 %collective-permute-start.1 = (bf16[128,12,48]{0,2,1:T(8,128)(2,1)S(1)}, bf16[128,12,48]{0,2,1:T(8,128)(2,1)S(1)}, u32[]{:S(2)}, u32[]{:S(2)}) collective-permute-start(bf16[128,12,48]{0,2,1:T(8,128)(2,1)S(1)} %get-tuple-element.7), channel_id=1, source_target_pairs={{0,14},{2,0},{4,2},{6,4},{8,6},{10,8},{12,10},{14,12},{1,15},{3,1}... | collective-permute-start | bytes 442376 | tf_op jit(solution)/shard_map/ppermute | solution.py:38
  16.9 2.9 collective-permute-done
  19.8 3.5 %collective-permute-start.3 = (bf16[128,12,48]{0,2,1:T(8,128)(2,1)S(1)}, bf16[128,12,48]{0,2,1:T(8,128)(2,1)}, u32[]{:S(2)}, u32[]{:S(2)}) collective-permute-start(bf16[128,12,48]{0,2,1:T(8,128)(2,1)S(1)} %collective-permute-done.1), channel_id=1, source_target_pairs={{0,14},{2,0},{4,2},{6,4},{8,6},{10,8},{12,10},{14,12},{1,15},{3,1}... | collective-permute-start | bytes 442376 | tf_op jit(solution)/shard_map/ppermute | solution.py:38
  23.3 3.7 %collective-permute-done.2 = bf16[128,12,48]{0,2,1:T(8,128)(2,1)S(1)} collective-permute-done((bf16[128,12,48]{0,2,1:T(8,128)(2,1)S(1)}, bf16[128,12,48]{0,2,1:T(8,128)(2,1)S(1)}, u32[]{:S(2)}, u32[]{:S(2)}) %collective-permute-start.2) | collective-permute-done | bytes 147488 | tf_op jit(solution)/shard_map/ppermute | solution.py:33
  27.0 3.7 %collective-permute-start.5 = (bf16[128,12,48]{0,2,1:T(8,128)(2,1)}, bf16[128,12,48]{0,2,1:T(8,128)(2,1)}, u32[]{:S(2)}, u32[]{:S(2)}) collective-permute-start(bf16[128,12,48]{0,2,1:T(8,128)(2,1)} %collective-permute-done.3), channel_id=1, source_target_pairs={{0,14},{2,0},{4,2},{6,4},{8,6},{10,8},{12,10},{14,12},{1,15},{3,1}... | collective-permute-start | bytes 442376 | tf_op jit(solution)/shard_map/ppermute | solution.py:38
  30.7 3.5 %collective-permute-done.4 = bf16[128,12,48]{0,2,1:T(8,128)(2,1)} collective-permute-done((bf16[128,12,48]{0,2,1:T(8,128)(2,1)S(1)}, bf16[128,12,48]{0,2,1:T(8,128)(2,1)}, u32[]{:S(2)}, u32[]{:S(2)}) %collective-permute-start.4) | collective-permute-done | bytes 147488 | tf_op jit(solution)/shard_map/ppermute | solution.py:33
  34.3 1.0 copy.112
  35.4 1.2 copy.120
  36.8 9.3 %dynamic_update_slice.24 = bf16[128,96,48]{1,2,0:T(8,128)(2,1)S(1)} dynamic-update-slice(bf16[128,96,48]{1,2,0:T(8,128)(2,1)S(1)} %broadcast_in_dim.2, bf16[128,12,48]{1,2,0:T(8,128)(2,1)S(1)} %copy.112, s32[]{:T(128)} %constant.81.clone.1, s32[]{:T(128)S(6)} %select_n.55, s32[]{:T(128)} %constant.81.clone.1) | dynamic-update-slice | bytes 294916 | tf_op jit(solution)/shard_map/dynamic_update_slice | solution.py:29
  46.1 1.9 copy.113
  48.0 28.4 %dynamic_update_slice.25 = bf16[128,96,48]{1,2,0:T(8,128)(2,1)S(1)} dynamic-update-slice(bf16[128,96,48]{1,2,0:T(8,128)(2,1)S(1)} %dynamic_update_slice.24, bf16[128,12,48]{1,2,0:T(8,128)(2,1)S(1)} %copy.113, s32[]{:T(128)} %constant.81.clone.1, s32[]{:T(128)S(6)} %select_n.57, s32[]{:T(128)} %constant.81.clone.1) | dynamic-update-slice | bytes 294916 | tf_op jit(solution)/shard_map/dynamic_update_slice | solution.py:34
  76.4 1.9 copy.114
  78.3 28.4 %dynamic_update_slice.26 = bf16[128,96,48]{1,2,0:T(8,128)(2,1)S(1)} dynamic-update-slice(bf16[128,96,48]{1,2,0:T(8,128)(2,1)S(1)} %dynamic_update_slice.25, bf16[128,12,48]{1,2,0:T(8,128)(2,1)S(1)} %copy.114, s32[]{:T(128)} %constant.81.clone.1, s32[]{:T(128)S(6)} %select_n.59, s32[]{:T(128)} %constant.81.clone.1) | dynamic-update-slice | bytes 294916 | tf_op jit(solution)/shard_map/dynamic_update_slice | solution.py:39
  106.7 1.9 copy.115
  108.7 28.4 %dynamic_update_slice.27 = bf16[128,96,48]{1,2,0:T(8,128)(2,1)S(1)} dynamic-update-slice(bf16[128,96,48]{1,2,0:T(8,128)(2,1)S(1)} %dynamic_update_slice.26, bf16[128,12,48]{1,2,0:T(8,128)(2,1)S(1)} %copy.115, s32[]{:T(128)} %constant.81.clone.1, s32[]{:T(128)S(6)} %select_n.61, s32[]{:T(128)} %constant.81.clone.1) | dynamic-update-slice | bytes 294916 | tf_op jit(solution)/shard_map/dynamic_update_slice | solution.py:34
  137.1 1.9 copy.116
  139.0 28.4 %dynamic_update_slice.28 = bf16[128,96,48]{1,2,0:T(8,128)(2,1)S(1)} dynamic-update-slice(bf16[128,96,48]{1,2,0:T(8,128)(2,1)S(1)} %dynamic_update_slice.27, bf16[128,12,48]{1,2,0:T(8,128)(2,1)S(1)} %copy.116, s32[]{:T(128)} %constant.81.clone.1, s32[]{:T(128)S(6)} %select_n.63, s32[]{:T(128)} %constant.81.clone.1) | dynamic-update-slice | bytes 294916 | tf_op jit(solution)/shard_map/dynamic_update_slice | solution.py:39
  167.4 1.9 copy.117
  169.3 28.4 %dynamic_update_slice.29 = bf16[128,96,48]{1,2,0:T(8,128)(2,1)S(1)} dynamic-update-slice(bf16[128,96,48]{1,2,0:T(8,128)(2,1)S(1)} %dynamic_update_slice.28, bf16[128,12,48]{1,2,0:T(8,128)(2,1)S(1)} %copy.117, s32[]{:T(128)} %constant.81.clone.1, s32[]{:T(128)S(6)} %select_n.65, s32[]{:T(128)} %constant.81.clone.1) | dynamic-update-slice | bytes 294916 | tf_op jit(solution)/shard_map/dynamic_update_slice | solution.py:34
  197.7 1.9 copy.118
  199.6 28.4 %dynamic_update_slice.30 = bf16[128,96,48]{1,2,0:T(8,128)(2,1)S(1)} dynamic-update-slice(bf16[128,96,48]{1,2,0:T(8,128)(2,1)S(1)} %dynamic_update_slice.29, bf16[128,12,48]{1,2,0:T(8,128)(2,1)S(1)} %copy.118, s32[]{:T(128)} %constant.81.clone.1, s32[]{:T(128)S(6)} %select_n.67, s32[]{:T(128)} %constant.81.clone.1) | dynamic-update-slice | bytes 294916 | tf_op jit(solution)/shard_map/dynamic_update_slice | solution.py:39
  228.0 1.9 copy.119
  230.0 28.6 %dynamic_update_slice.31 = bf16[128,96,48]{1,2,0:T(8,128)(2,1)S(1)} dynamic-update-slice(bf16[128,96,48]{1,2,0:T(8,128)(2,1)S(1)} %dynamic_update_slice.30, bf16[128,12,48]{1,2,0:T(8,128)(2,1)S(1)} %copy.119, s32[]{:T(128)} %constant.81.clone.1, s32[]{:T(128)S(6)} %select_n.69, s32[]{:T(128)} %constant.81.clone.1) | dynamic-update-slice | bytes 294916 | tf_op jit(solution)/shard_map/dynamic_update_slice | solution.py:34
  258.6 1.6 fusion.76
  260.2 1.5 copy.121
  262.2 19.1 %reduce-scatter.2.cloned.1.call-done = f32[128,12,48]{0,1,2:T(8,128)} async-done(((f32[128,12,96]{0,1,2:T(8,128)}), f32[128,12,48]{0,1,2:T(8,128)}) %reduce-scatter.2.cloned.1.call-update) | async-done | bytes 294928 | tf_op jit(solution)/shard_map/reduce_scatter | solution.py:80
  281.3 1.2 reduce_sum.92
  282.7 1.3 multiply_reduce_fusion.1
  284.2 1.3 multiply_convert_fusion.1
  286.1 0.4 convolution_bitcast_fusion
  286.5 0.9 fusion.24
  287.3 6.1 %all_gather.6 = bf16[128,12,96]{0,2,1:T(8,128)(2,1)S(1)} all-gather(bf16[128,12,48]{0,2,1:T(8,128)(2,1)S(1)} %get-tuple-element.6), channel_id=1, replica_groups=mesh['grp'=2,'row'=8,'col'=2] {'col'}, dimensions={2}, use_global_device_ids=true | all-gather | bytes 442368 | tf_op jit(solution)/shard_map/all_gather | solution.py:83
  293.4 0.9 copy.130
  294.3 4.6 %all-to-all-start = ((bf16[128,12,96]{0,1,2:T(8,128)(2,1)}), bf16[128,12,96]{0,1,2:T(8,128)(2,1)S(1)}, u32[]{:S(2)}, u32[]{:S(2)}) async-start(bf16[128,12,96]{0,1,2:T(8,128)(2,1)} %copy.130), calls=%async_computation.1 | async-start | bytes 786432 | tf_op jit(solution)/shard_map/all_to_all | solution.py:84
  298.9 1.1 fusion.8
  300.0 17.1 %all-to-all-done = bf16[128,12,96]{0,1,2:T(8,128)(2,1)S(1)} async-done(((bf16[128,12,96]{0,1,2:T(8,128)(2,1)}), bf16[128,12,96]{0,1,2:T(8,128)(2,1)S(1)}, u32[]{:S(2)}, u32[]{:S(2)}) %all-to-all-start) | async-done | bytes 294944 | tf_op jit(solution)/shard_map/all_to_all | solution.py:84
  317.2 1.2 copy.133
  318.4 5.3 %copy.134 = bf16[128,96,48]{2,1,0:T(8,128)(2,1)S(1)} copy(bf16[128,96,48]{0,2,1:T(8,128)(2,1)} %all-gather.2.cloned.1.call-done) | data formatting | bytes 2359296 | tf_op jit(solution)/shard_map/all_gather | solution.py:86
  323.7 2.0 fusion.74
  326.1 0.6 copy-done.2
  326.8 0.4 fusion.75
  327.5 0.5 fusion.53
  328.1 1.1 fusion.14
  (66 shorter events, 3.0 us)
Async XLA Ops:
  6.5 320.9 %copy-start = (bf16[128,1024]{1,0:T(8,128)(2,1)S(1)}, bf16[128,1024]{1,0:T(8,128)(2,1)}, u32[]{:S(2)}) copy-start(bf16[128,1024]{1,0:T(8,128)(2,1)} %param.12) | copy-start | bytes 786436
  6.5 274.8 %reduce-scatter.2.cloned.1.call-start = ((), (), s32[]{:S(2)}) async-start(), calls=%async_computation.2 | async-start | bytes 1179648 | tf_op jit(solution)/shard_map/reduce_scatter | solution.py:80
  9.5 2.7 copy-start.9
  12.2 7.5 %collective-permute-start = (bf16[128,12,48]{0,2,1:T(8,128)(2,1)S(1)}, bf16[128,12,48]{0,2,1:T(8,128)(2,1)S(1)}, u32[]{:S(2)}, u32[]{:S(2)}) collective-permute-start(bf16[128,12,48]{0,2,1:T(8,128)(2,1)S(1)} %get-tuple-element.7), channel_id=1, source_target_pairs={{0,2},{2,4},{4,6},{6,8},{8,10},{10,12},{12,14},{14,0},{1,3},{3,5},... | collective-permute-start | bytes 442376 | tf_op jit(solution)/shard_map/ppermute | solution.py:33
  12.8 7.0 %collective-permute-start.1 = (bf16[128,12,48]{0,2,1:T(8,128)(2,1)S(1)}, bf16[128,12,48]{0,2,1:T(8,128)(2,1)S(1)}, u32[]{:S(2)}, u32[]{:S(2)}) collective-permute-start(bf16[128,12,48]{0,2,1:T(8,128)(2,1)S(1)} %get-tuple-element.7), channel_id=1, source_target_pairs={{0,14},{2,0},{4,2},{6,4},{8,6},{10,8},{12,10},{14,12},{1,15},{3,1}... | collective-permute-start | bytes 442376 | tf_op jit(solution)/shard_map/ppermute | solution.py:38
  19.7 16.8 %copy-start.7 = (bf16[128,12,48]{0,2,1:T(8,128)(2,1)}, bf16[128,12,48]{0,2,1:T(8,128)(2,1)S(1)}, u32[]{:S(2)}) copy-start(bf16[128,12,48]{0,2,1:T(8,128)(2,1)S(1)} %collective-permute-done) | copy-start | bytes 442372
  19.7 7.2 %collective-permute-start.2 = (bf16[128,12,48]{0,2,1:T(8,128)(2,1)S(1)}, bf16[128,12,48]{0,2,1:T(8,128)(2,1)S(1)}, u32[]{:S(2)}, u32[]{:S(2)}) collective-permute-start(bf16[128,12,48]{0,2,1:T(8,128)(2,1)S(1)} %collective-permute-done), channel_id=1, source_target_pairs={{0,2},{2,4},{4,6},{6,8},{8,10},{10,12},{12,14},{14,0},{1,3},{3,5},... | collective-permute-start | bytes 442376 | tf_op jit(solution)/shard_map/ppermute | solution.py:33
  19.7 16.8 %copy-start.5 = (bf16[128,12,48]{0,2,1:T(8,128)(2,1)}, bf16[128,12,48]{0,2,1:T(8,128)(2,1)S(1)}, u32[]{:S(2)}) copy-start(bf16[128,12,48]{0,2,1:T(8,128)(2,1)S(1)} %collective-permute-done.1) | copy-start | bytes 442372
  19.8 7.2 %collective-permute-start.3 = (bf16[128,12,48]{0,2,1:T(8,128)(2,1)S(1)}, bf16[128,12,48]{0,2,1:T(8,128)(2,1)}, u32[]{:S(2)}, u32[]{:S(2)}) collective-permute-start(bf16[128,12,48]{0,2,1:T(8,128)(2,1)S(1)} %collective-permute-done.1), channel_id=1, source_target_pairs={{0,14},{2,0},{4,2},{6,4},{8,6},{10,8},{12,10},{14,12},{1,15},{3,1}... | collective-permute-start | bytes 442376 | tf_op jit(solution)/shard_map/ppermute | solution.py:38
  27.0 9.6 %copy-start.6 = (bf16[128,12,48]{0,2,1:T(8,128)(2,1)}, bf16[128,12,48]{0,2,1:T(8,128)(2,1)S(1)}, u32[]{:S(2)}) copy-start(bf16[128,12,48]{0,2,1:T(8,128)(2,1)S(1)} %collective-permute-done.2) | copy-start | bytes 442372
  27.0 7.3 %collective-permute-start.4 = (bf16[128,12,48]{0,2,1:T(8,128)(2,1)S(1)}, bf16[128,12,48]{0,2,1:T(8,128)(2,1)}, u32[]{:S(2)}, u32[]{:S(2)}) collective-permute-start(bf16[128,12,48]{0,2,1:T(8,128)(2,1)S(1)} %collective-permute-done.2), channel_id=1, source_target_pairs={{0,2},{2,4},{4,6},{6,8},{8,10},{10,12},{12,14},{14,0},{1,3},{3,5},... | collective-permute-start | bytes 442376 | tf_op jit(solution)/shard_map/ppermute | solution.py:33
  27.0 170.7 %collective-permute-start.5 = (bf16[128,12,48]{0,2,1:T(8,128)(2,1)}, bf16[128,12,48]{0,2,1:T(8,128)(2,1)}, u32[]{:S(2)}, u32[]{:S(2)}) collective-permute-start(bf16[128,12,48]{0,2,1:T(8,128)(2,1)} %collective-permute-done.3), channel_id=1, source_target_pairs={{0,14},{2,0},{4,2},{6,4},{8,6},{10,8},{12,10},{14,12},{1,15},{3,1}... | collective-permute-start | bytes 442376 | tf_op jit(solution)/shard_map/ppermute | solution.py:38
  34.3 193.8 %collective-permute-start.6 = (bf16[128,12,48]{0,2,1:T(8,128)(2,1)}, bf16[128,12,48]{0,2,1:T(8,128)(2,1)}, u32[]{:S(2)}, u32[]{:S(2)}) collective-permute-start(bf16[128,12,48]{0,2,1:T(8,128)(2,1)} %collective-permute-done.4), channel_id=1, source_target_pairs={{0,2},{2,4},{4,6},{6,8},{8,10},{10,12},{12,14},{14,0},{1,3},{3,5},... | collective-permute-start | bytes 442376 | tf_op jit(solution)/shard_map/ppermute | solution.py:33
  260.1 1.7 copy-start.3
  260.1 1.7 copy-start.10
  260.1 1.7 copy-start.12
  261.6 56.8 %all-gather.2.cloned.1.call-start = ((), (), s32[]{:S(2)}) async-start(), calls=%async_computation.3 | async-start | bytes 1327104 | tf_op jit(solution)/shard_map/all_gather | solution.py:86
  261.9 23.6 %copy-start.8 = (bf16[2,128,128]{2,1,0:T(8,128)(2,1)S(1)}, bf16[2,128,128]{2,1,0:T(8,128)(2,1)}, u32[]{:S(2)}) copy-start(bf16[2,128,128]{2,1,0:T(8,128)(2,1)} %param.11) | copy-start | bytes 196612
  285.8 13.2 %copy-start.1 = (f32[12,48,128]{2,1,0:T(8,128)}, f32[12,48,128]{2,1,0:T(8,128)S(1)}, u32[]{:S(2)}) copy-start(f32[12,48,128]{2,1,0:T(8,128)S(1)} %get-tuple-element.12) | copy-start | bytes 884740
  294.3 22.8 %all-to-all-start = ((bf16[128,12,96]{0,1,2:T(8,128)(2,1)}), bf16[128,12,96]{0,1,2:T(8,128)(2,1)S(1)}, u32[]{:S(2)}, u32[]{:S(2)}) async-start(bf16[128,12,96]{0,1,2:T(8,128)(2,1)} %copy.130), calls=%async_computation.1 | async-start | bytes 786432 | tf_op jit(solution)/shard_map/all_to_all | solution.py:84
  325.7 1.0 copy-start.2
  325.7 1.0 copy-start.4
  327.2 0.9 copy-start.11
Sparse Core Ops, SparseCore 0:
  261.8 19.5 reduce-scatter.1
  287.5 30.0 all-gather.1
